TPU v7x, 512 devices: a whole 4x8x8 slice. The times are simulated.
512 devices in a mesh: tensor: 64 (over x, y, core), replica: 8 (over z).
Axes of the slice: x: 4, y: 8, z: 8, core: 2. Of those that a mesh axis runs over, the one named last changes fastest.
Arguments:
- amplitudes: bfloat16 [1024, 64, 128], P('tensor'), may hold values from -6 to 6
- block_slot: int32 [1024], replicated, may hold values from 0 to 1023, each once
- integrals: bfloat16 [1024, 64, 64, 64], P('tensor', 'replica'), may hold values from -0.09375 to 0.09375
- tile_cols: int32 [1024, 64], P('tensor'), may hold values from 0 to 1023, as said below
- irreps: int32 [1024], replicated, may hold values from 0 to 7, as said below
Outputs:
- ladder: float32 [1024, 64, 128], P('tensor', None, 'replica')
Inputs may be any that keep to these rules, and one draw needn't show every extreme that they name: `block_slot`: each block has one slot and each slot one block. `tile_cols`: the tiles of a row that name blocks of the row's own irrep name distinct blocks; other tiles may name any block of another irrep. `irreps`: each irrep labels exactly 128 blocks.
All inputs are finite; a program needn't handle non-finite values.
Results may differ from a plain program's by a relative error of at most 0.0003.
Values may be sent and summed in bfloat16 or wider, within the bound.
No kernel may reach another device: no remote copies, remote signals or barrier semaphores. Data moves between devices by JAX's collectives and lax.ppermute only.
A program may use at most 128 MiB of HBM per device.

v0:
```python
import jax
import jax.numpy as jnp
from jax import lax
from jax.sharding import PartitionSpec as P


def local(amplitudes, block_slot, integrals, tile_cols, irreps):
    blocks = tile_cols.shape[0]
    rep_id = lax.axis_index("replica")
    rows_glob = lax.axis_index("tensor") * blocks + jnp.arange(blocks, dtype=jnp.int32)
    row_irrep = irreps[rows_glob]
    per_rep = integrals.shape[1]
    my_cols = lax.dynamic_slice_in_dim(tile_cols, rep_id * per_rep, per_rep, 1)
    whole = lax.all_gather(amplitudes, "tensor", axis=0, tiled=True)
    picked = whole[block_slot[my_cols]]
    allowed = (irreps[my_cols] == row_irrep[:, None]).astype(jnp.bfloat16)
    tiles = integrals * allowed[:, :, None, None]
    partial_sum = jnp.einsum("bnxy,bnyp->bxp", tiles, picked, preferred_element_type=jnp.float32)
    return lax.psum_scatter(partial_sum, "replica", scatter_dimension=2, tiled=True)


def solution(mesh):
    in_specs = (
        P("tensor", None, None),
        P(),
        P("tensor", "replica", None, None),
        P("tensor", None),
        P(),
    )
    out_specs = P("tensor", None, "replica")
    return jax.shard_map(local, mesh=mesh, in_specs=in_specs, out_specs=out_specs, check_vma=False)
```

profile of v0, /device:TPU:2, one launch (start us, length us, event | category | flops | bytes accessed | tf_op | source)
XLA Modules:
  0.0 177.6 jit_solution(1262501762788884398)
XLA Ops:
  6.5 0.0 copy-start
  6.5 0.0 all-gather.2.cloned.1.call-start
  6.5 0.7 all-gather.2.cloned.1.call-update
  7.3 0.0 reduce-scatter.2.cloned.1.call-start
  7.3 0.8 compare_select_fusion.1
  8.1 0.1 reshape.50
  8.2 0.0 copy-done
  8.2 0.6 gather_fusion.1
  8.9 0.0 copy-start.1
  8.9 1.0 gather_fusion
  9.9 0.0 copy-done.1
  9.9 1.0 gather_fusion.2
  10.8 0.1 reshape.49
  10.9 0.1 gather.17
  11.0 0.1 reshape.74
  11.1 0.1 compare_convert_fusion
  11.2 107.2 %all-gather.2.cloned.1.call-done = bf16[1024,64,128]{2,1,0:T(8,128)(2,1)} async-done(((bf16[16,64,128]{2,1,0:T(8,128)(2,1)}), bf16[1024,64,128]{2,1,0:T(8,128)(2,1)}) %all-gather.2.cloned.1.call-update) | async-done | bytes 16777232 | tf_op jit(solution)/shard_map/all_gather | solution.py:14
  118.4 6.7 %gather_fusion.3 = bf16[128,64,128]{2,1,0:T(8,128)(2,1)S(1)} fusion(bf16[1024,64,128]{2,1,0:T(8,128)(2,1)} %all-gather.2.cloned.1.call-done, s32[1024]{0:T(1024)S(1)} %pad_clamp_fusion), kind=kCustom, calls=%fused_computation.3 | custom fusion | bytes 4194816 | tf_op jit(solution)/shard_map/gather | solution.py:15
  125.2 4.1 %fusion.2 = f32[16,64,128]{1,2,0:T(8,128)} fusion(bf16[16,8,64,128]{3,2,1,0:T(8,128)(2,1)S(1)} %bitcast.9, bf16[16,8,64,64]{3,2,1,0:T(8,128)(2,1)} %param.7, bf16[16,8]{1,0:T(8,128)(2,1)S(1)} %compare_convert_fusion), kind=kOutput, calls=%fused_computation.6 | convolution fusion | flops 134742016 | bytes 3670272 | tf_op jit(solution)/shard_map/bnxy,bnyp->bxp/dot_general | solution.py:18
  129.3 0.0 reduce-scatter.2.cloned.1.call-update
  129.3 41.4 %reduce-scatter.2.cloned.1.call-done = f32[16,64,16]{1,2,0:T(8,128)} async-done(((f32[16,64,128]{1,2,0:T(8,128)}), f32[16,64,16]{1,2,0:T(8,128)}) %reduce-scatter.2.cloned.1.call-update) | async-done | bytes 65552 | tf_op jit(solution)/shard_map/reduce_scatter | solution.py:19
  (5 shorter events, 0.0 us)
Async XLA Ops:
  6.5 1.7 copy-start
  6.5 111.9 %all-gather.2.cloned.1.call-start = ((), (), s32[]{:S(2)}) async-start(), calls=%async_computation.1 | async-start | bytes 17039360 | tf_op jit(solution)/shard_map/all_gather | solution.py:14
  7.3 163.5 %reduce-scatter.2.cloned.1.call-start = ((), (), s32[]{:S(2)}) async-start(), calls=%async_computation.2 | async-start | bytes 1179648 | tf_op jit(solution)/shard_map/reduce_scatter | solution.py:19
  8.9 1.0 copy-start.1
Sparse Core Ops, SparseCore 0:
  10.7 107.6 all-gather.1
  129.4 41.2 reduce-scatter.1
where the time goes:
time: 178 us
  waiting for transfers between devices  149 us (84%)
  between operations  13.5 us (8%)
  local copies, waits for them, and re-layouts  9.65 us (5%)
  matrix products  4.12 us (2%)
    all_gather x1, waiting for transfers between devices, local(): whole = lax.all_gather(amplitudes, 'tensor', axis=0, tiled=True)  107 us
    reduce_scatter x1, waiting for transfers between devices, local(): lax.psum_scatter(partial_sum, 'replica', scatter_dimension=2, tiled=True)  41.4 us
    gather x3, local copies, waits for them, and re-layouts, local(): picked = whole[block_slot[my_cols]]  7.77 us
    dot_general x1, matrix products, local(): jnp.einsum('bnxy,bnyp->bxp', tiles, picked, preferred_element_type=jnp.fl...  4.12 us
  transfers between devices with their start and end apart: 2, of which 2 were waited for; matrix products, arithmetic and copies ran while one was open for 2% of the time, Pallas kernels for 0%

commit v1 on v0

--- a/solution.py
+++ b/solution.py
@@ -11,7 +11,11 @@
     row_irrep = irreps[rows_glob]
     per_rep = integrals.shape[1]
     my_cols = lax.dynamic_slice_in_dim(tile_cols, rep_id * per_rep, per_rep, 1)
-    whole = lax.all_gather(amplitudes, "tensor", axis=0, tiled=True)
+    peers = lax.axis_size("tensor")
+    repeats = [peers if d == 0 else 1 for d in range(amplitudes.ndim)]
+    whole = lax.all_to_all(
+        jnp.tile(amplitudes, repeats), "tensor", split_axis=0, concat_axis=0, tiled=True
+    )
     picked = whole[block_slot[my_cols]]
     allowed = (irreps[my_cols] == row_irrep[:, None]).astype(jnp.bfloat16)
     tiles = integrals * allowed[:, :, None, None]

time: 178 us -> 451 us (2.53)
  the two profiles are of different devices: /device:TPU:2 before, /device:TPU:4 now
where the time goes in v1:
time: 451 us; the launch traced here: 450 us
  waiting for transfers between devices  404 us (90%)
  local copies, waits for them, and re-layouts  17 us (4%)
  between operations  13.5 us (3%)
  starting transfers between devices  11.5 us (3%)
    all_to_all x1, waiting for transfers between devices, local(): lax.all_to_all(jnp.tile(amplitudes, repeats), 'tensor', split_axis=0, con...  358 us
    reduce_scatter x1, waiting for transfers between devices, local(): lax.psum_scatter(partial_sum, 'replica', scatter_dimension=2, tiled=True)  45.4 us
    all_to_all x1, starting transfers between devices, local(): lax.all_to_all(jnp.tile(amplitudes, repeats), 'tensor', split_axis=0, con...  11.4 us
  transfers between devices with their start and end apart: 2, of which 2 were waited for; matrix products, arithmetic and copies ran while one was open for 1% of the time, Pallas kernels for 0%

profile of v1, /device:TPU:4, one launch (start us, length us, event | category | flops | bytes accessed | tf_op | source)
XLA Modules:
  0.0 450.2 jit_solution(12165860627065780339)
XLA Ops:
  6.5 0.0 copy-start
  6.5 6.9 %tile.4 = bf16[64,16,64,128]{3,2,1,0:T(8,128)(2,1)} broadcast(bf16[16,64,128]{2,1,0:T(8,128)(2,1)} %param.5), dimensions={1,2,3} | broadcast | bytes 17039360 | tf_op jit(solution)/shard_map/tile | solution.py:17
  13.5 0.0 copy-start.2
  13.5 11.4 %all-to-all-start = ((bf16[1024,64,128]{2,1,0:T(8,128)(2,1)}), bf16[1024,64,128]{2,1,0:T(8,128)(2,1)}, u32[]{:S(2)}, u32[]{:S(2)}) async-start(bf16[1024,64,128]{2,1,0:T(8,128)(2,1)} %bitcast.10), calls=%async_computation | async-start | bytes 33554432 | tf_op jit(solution)/shard_map/all_to_all | solution.py:16
  24.9 0.0 copy-start.1
  24.9 0.0 reduce-scatter.2.cloned.1.call-start
  25.0 0.0 copy-done.2
  25.0 0.1 compare_select_fusion.1
  25.1 0.1 reshape.54
  25.2 0.4 copy-done.1
  25.6 1.0 gather_fusion.2
  26.6 0.1 gather.17
  26.7 0.1 reshape.78
  26.8 0.0 copy-done
  26.8 1.0 gather_fusion
  27.8 0.1 reshape.53
  27.9 0.6 gather_fusion.1
  28.5 0.1 compare_convert_fusion
  28.6 358.5 %all-to-all-done = bf16[1024,64,128]{2,1,0:T(8,128)(2,1)} async-done(((bf16[1024,64,128]{2,1,0:T(8,128)(2,1)}), bf16[1024,64,128]{2,1,0:T(8,128)(2,1)}, u32[]{:S(2)}, u32[]{:S(2)}) %all-to-all-start) | async-done | bytes 16777248 | tf_op jit(solution)/shard_map/all_to_all | solution.py:16
  387.1 6.7 %gather_fusion.3 = bf16[128,64,128]{2,1,0:T(8,128)(2,1)S(1)} fusion(bf16[1024,64,128]{2,1,0:T(8,128)(2,1)} %all-to-all-done, s32[1024]{0:T(1024)S(1)} %pad_clamp_fusion), kind=kCustom, calls=%fused_computation.3 | custom fusion | bytes 4194816 | tf_op jit(solution)/shard_map/gather | solution.py:19
  393.8 4.1 fusion.2
  397.9 0.0 reduce-scatter.2.cloned.1.call-update
  397.9 45.4 %reduce-scatter.2.cloned.1.call-done = f32[16,64,16]{1,2,0:T(8,128)} async-done(((f32[16,64,128]{1,2,0:T(8,128)}), f32[16,64,16]{1,2,0:T(8,128)}) %reduce-scatter.2.cloned.1.call-update) | async-done | bytes 65552 | tf_op jit(solution)/shard_map/reduce_scatter | solution.py:23
  (5 shorter events, 0.0 us)
Async XLA Ops:
  6.5 20.2 %copy-start = (s32[1024]{0:T(1024)S(1)}, s32[1024]{0:T(1024)}, u32[]{:S(2)}) copy-start(s32[1024]{0:T(1024)} %param.9) | copy-start | bytes 12292
  13.5 11.5 %copy-start.2 = (s32[16,64]{1,0:T(8,128)S(1)}, s32[16,64]{1,0:T(8,128)}, u32[]{:S(2)}) copy-start(s32[16,64]{1,0:T(8,128)} %param.8) | copy-start | bytes 12292
  13.5 373.6 %all-to-all-start = ((bf16[1024,64,128]{2,1,0:T(8,128)(2,1)}), bf16[1024,64,128]{2,1,0:T(8,128)(2,1)}, u32[]{:S(2)}, u32[]{:S(2)}) async-start(bf16[1024,64,128]{2,1,0:T(8,128)(2,1)} %bitcast.10), calls=%async_computation | async-start | bytes 33554432 | tf_op jit(solution)/shard_map/all_to_all | solution.py:16
  24.9 0.7 copy-start.1
  24.9 418.4 %reduce-scatter.2.cloned.1.call-start = ((), (), s32[]{:S(2)}) async-start(), calls=%async_computation.2 | async-start | bytes 1179648 | tf_op jit(solution)/shard_map/reduce_scatter | solution.py:23
Sparse Core Ops, SparseCore 0:
  398.1 45.2 reduce-scatter.1
